TPU v7x, 32 devices: a whole 2x2x4 slice. The times are simulated.
32 devices in a mesh: wide: 8 (over z, y), narrow: 4 (over x, core).
Axes of the slice: x: 2, y: 2, z: 4, core: 2. Of those that a mesh axis runs over, the one named last changes fastest.
Arguments:
- tokens: bfloat16 [64, 600, 768], P(('wide', 'narrow')), may hold values from -6 to 6
- lengths: int32 [64], P(('wide', 'narrow')), may hold values from 256 to 600, as said below
- blocks: int32 [64, 600], P(('wide', 'narrow')), may hold values from 0 to 4, never falling along the last dimension, each value on 1 to 300 neighbouring positions
- ln1_gain: bfloat16 [768], P(('wide', 'narrow')), may hold values from 0.25 to 1.75
- ln1_bias: bfloat16 [768], P(('wide', 'narrow')), may hold values from -1.75 to 1.75
- qkv_weight: bfloat16 [768, 2304], P(('wide', 'narrow')), may hold values from -0.3125 to 0.3125
- qv_bias: bfloat16 [1536], P(('wide', 'narrow')), may hold values from -1.75 to 1.75
- out_weight: bfloat16 [768, 768], P(('wide', 'narrow')), may hold values from -1.25 to 1.25
- out_bias: bfloat16 [768], P(('wide', 'narrow')), may hold values from -1.75 to 1.75
- ln2_gain: bfloat16 [768], P(('wide', 'narrow')), may hold values from 0.25 to 1.75
- ln2_bias: bfloat16 [768], P(('wide', 'narrow')), may hold values from -1.75 to 1.75
- up_weight: bfloat16 [768, 3072], P(('wide', 'narrow')), may hold values from -0.21875 to 0.21875
- up_bias: bfloat16 [3072], P(('wide', 'narrow')), may hold values from -1.75 to 1.75
- down_weight: bfloat16 [3072, 768], P(('wide', 'narrow')), may hold values from -0.109375 to 0.109375
- down_bias: bfloat16 [768], P(('wide', 'narrow')), may hold values from -1.75 to 1.75
- cotangent: bfloat16 [64, 600, 768], P(('wide', 'narrow')), may hold values from -12 to 12
Outputs:
- output: bfloat16 [64, 600, 768], P(('wide', 'narrow'))
- input_grad: float32 [64, 600, 768], P(('wide', 'narrow'))
- ln1_gain_grad: float32 [768], P(('wide', 'narrow'))
- ln1_bias_grad: float32 [768], P(('wide', 'narrow'))
- qkv_weight_grad: float32 [768, 2304], P(('wide', 'narrow'))
- qv_bias_grad: float32 [1536], P(('wide', 'narrow'))
- out_weight_grad: float32 [768, 768], P(('wide', 'narrow'))
- out_bias_grad: float32 [768], P(('wide', 'narrow'))
- ln2_gain_grad: float32 [768], P(('wide', 'narrow'))
- ln2_bias_grad: float32 [768], P(('wide', 'narrow'))
- up_weight_grad: float32 [768, 3072], P(('wide', 'narrow'))
- up_bias_grad: float32 [3072], P(('wide', 'narrow'))
- down_weight_grad: float32 [3072, 768], P(('wide', 'narrow'))
- down_bias_grad: float32 [768], P(('wide', 'narrow'))
Inputs may be any that keep to these rules, and one draw needn't show every extreme that they name: Slots at and after lengths[b] of item b are padding; some item has 600 real tokens and some 256. `blocks`: block ids of an item start at 0 at slot 0 and never fall along the slots.
All inputs are finite; a program needn't handle non-finite values.
Results may differ from a plain program's by a relative error of at most 0.012.
The roundings to bfloat16 on the way count: a program that leaves them out, or rounds other values in their place, can miss the bound.
Values may be sent and summed in bfloat16 or wider, within the bound.
No kernel may reach another device: no remote copies, remote signals or barrier semaphores. Data moves between devices by JAX's collectives and lax.ppermute only.
A program may use at most 256 MiB of HBM per device.

v0:
```python
from functools import partial
import jax
import jax.numpy as jnp
from jax import lax
from jax.sharding import PartitionSpec as P

D = 768
HEADS = 12
HEAD = 64
norm_epsilon = 1e-05
masked_score = -1e30


def layer_norm(values, gain, shift):
    centred = values - jnp.mean(values, axis=-1, keepdims=True)
    inverse = lax.rsqrt(jnp.mean(centred * centred, axis=-1, keepdims=True) + norm_epsilon)
    scaled = centred * inverse
    return (scaled * gain + shift, scaled, inverse)


def norm_back(d_normed, scaled, inverse, gain):
    gain_grad = jnp.sum(d_normed * scaled, axis=0)
    shift_grad = jnp.sum(d_normed, axis=0)
    d_scaled = d_normed * gain
    centre_term = jnp.mean(d_scaled, axis=-1, keepdims=True)
    slope_term = jnp.mean(d_scaled * scaled, axis=-1, keepdims=True)
    return (inverse * (d_scaled - centre_term - scaled * slope_term), gain_grad, shift_grad)


def allowed_pairs(item_length, block_ids):
    slot_count = block_ids.shape[0]
    column = lax.broadcasted_iota(jnp.int32, (slot_count, slot_count), 1)
    return (block_ids[None, :] <= block_ids[:, None]) & (column < item_length)


def head_split(packed, index):
    slot_count = packed.shape[0]
    return packed[:, index * D : (index + 1) * D].reshape(slot_count, HEADS, HEAD)


def score_table(queries, key_rows, allowed):
    scores = jnp.einsum(
        "qhd,khd->hqk", queries, key_rows, preferred_element_type=jnp.float32
    ) * HEAD ** (-0.5)
    return jnp.where(allowed[None], scores, masked_score)


def attend_forward(packed):
    qkv_item, item_length, block_ids = packed
    slot_count = qkv_item.shape[0]
    scores = score_table(
        head_split(qkv_item, 0), head_split(qkv_item, 1), allowed_pairs(item_length, block_ids)
    )
    peak_score = jnp.max(scores, axis=-1, keepdims=True)
    exponent = jnp.exp(scores - peak_score)
    row_total = jnp.sum(exponent, axis=-1, keepdims=True)
    probs_low = (exponent / row_total).astype(jnp.bfloat16)
    mixed_heads = jnp.einsum(
        "hqk,khd->qhd", probs_low, head_split(qkv_item, 2), preferred_element_type=jnp.float32
    )
    return (
        mixed_heads.reshape(slot_count, D).astype(jnp.bfloat16),
        peak_score + jnp.log(row_total),
    )


def attend_backward(packed):
    qkv_item, item_length, block_ids, log_total, d_mixed = packed
    slot_count = qkv_item.shape[0]
    queries = head_split(qkv_item, 0)
    key_rows = head_split(qkv_item, 1)
    value_rows = head_split(qkv_item, 2)
    scores = score_table(queries, key_rows, allowed_pairs(item_length, block_ids))
    probs = jnp.exp(scores - log_total)
    probs_low = probs.astype(jnp.bfloat16)
    d_heads = d_mixed.reshape(slot_count, HEADS, HEAD)
    d_values = jnp.einsum("hqk,qhd->khd", probs_low, d_heads, preferred_element_type=jnp.float32)
    d_probs = jnp.einsum("qhd,khd->hqk", d_heads, value_rows, preferred_element_type=jnp.float32)
    d_scores = (probs * (d_probs - jnp.sum(probs * d_probs, axis=-1, keepdims=True))).astype(
        jnp.bfloat16
    )
    d_queries = jnp.einsum(
        "hqk,khd->qhd", d_scores, key_rows, preferred_element_type=jnp.float32
    ) * HEAD ** (-0.5)
    d_keys = jnp.einsum(
        "hqk,qhd->khd", d_scores, queries, preferred_element_type=jnp.float32
    ) * HEAD ** (-0.5)
    joined = jnp.concatenate(
        [
            d_queries.reshape(slot_count, D),
            d_keys.reshape(slot_count, D),
            d_values.reshape(slot_count, D),
        ],
        axis=1,
    )
    return joined.astype(jnp.bfloat16)


def fetch(shards):
    (
        gain_one,
        shift_one,
        w_qkv,
        bias_qv,
        w_out,
        bias_out,
        gain_two,
        shift_two,
        w_up,
        bias_up,
        w_down,
        bias_down,
    ) = shards
    whole_set = (
        lax.all_gather(gain_one, ("wide", "narrow"), axis=0, tiled=True),
        lax.all_gather(shift_one, ("wide", "narrow"), axis=0, tiled=True),
        lax.all_gather(w_qkv, ("wide", "narrow"), axis=0, tiled=True),
        lax.all_gather(bias_qv, ("wide", "narrow"), axis=0, tiled=True),
        lax.all_gather(w_out, ("wide", "narrow"), axis=0, tiled=True),
        lax.all_gather(bias_out, ("wide", "narrow"), axis=0, tiled=True),
        lax.all_gather(gain_two, ("wide", "narrow"), axis=0, tiled=True),
        lax.all_gather(shift_two, ("wide", "narrow"), axis=0, tiled=True),
        lax.all_gather(w_up, ("wide", "narrow"), axis=0, tiled=True),
        lax.all_gather(bias_up, ("wide", "narrow"), axis=0, tiled=True),
        lax.all_gather(w_down, ("wide", "narrow"), axis=0, tiled=True),
        lax.all_gather(bias_down, ("wide", "narrow"), axis=0, tiled=True),
    )
    return whole_set


def reduce_grads(grads):
    (
        gain_one,
        shift_one,
        w_qkv,
        bias_qv,
        w_out,
        bias_out,
        gain_two,
        shift_two,
        w_up,
        bias_up,
        w_down,
        bias_down,
    ) = grads
    owned = (
        lax.psum_scatter(gain_one, ("wide", "narrow"), scatter_dimension=0, tiled=True),
        lax.psum_scatter(shift_one, ("wide", "narrow"), scatter_dimension=0, tiled=True),
        lax.psum_scatter(w_qkv, ("wide", "narrow"), scatter_dimension=0, tiled=True),
        lax.psum_scatter(bias_qv, ("wide", "narrow"), scatter_dimension=0, tiled=True),
        lax.psum_scatter(w_out, ("wide", "narrow"), scatter_dimension=0, tiled=True),
        lax.psum_scatter(bias_out, ("wide", "narrow"), scatter_dimension=0, tiled=True),
        lax.psum_scatter(gain_two, ("wide", "narrow"), scatter_dimension=0, tiled=True),
        lax.psum_scatter(shift_two, ("wide", "narrow"), scatter_dimension=0, tiled=True),
        lax.psum_scatter(w_up, ("wide", "narrow"), scatter_dimension=0, tiled=True),
        lax.psum_scatter(bias_up, ("wide", "narrow"), scatter_dimension=0, tiled=True),
        lax.psum_scatter(w_down, ("wide", "narrow"), scatter_dimension=0, tiled=True),
        lax.psum_scatter(bias_down, ("wide", "narrow"), scatter_dimension=0, tiled=True),
    )
    return tuple(owned)


def body(
    tokens,
    lengths,
    blocks,
    ln1_gain,
    ln1_bias,
    qkv_weight,
    qv_bias,
    out_weight,
    out_bias,
    ln2_gain,
    ln2_bias,
    up_weight,
    up_bias,
    down_weight,
    down_bias,
    cotangent,
):
    item_count, slot_count, model_width = tokens.shape
    row_count = item_count * slot_count
    shards = (
        ln1_gain,
        ln1_bias,
        qkv_weight,
        qv_bias,
        out_weight,
        out_bias,
        ln2_gain,
        ln2_bias,
        up_weight,
        up_bias,
        down_weight,
        down_bias,
    )
    layer_weights = fetch(shards)
    (
        gain_one,
        shift_one,
        w_qkv,
        bias_qv,
        w_out,
        bias_out,
        gain_two,
        shift_two,
        w_up,
        bias_up,
        w_down,
        bias_down,
    ) = layer_weights
    inputs = tokens.reshape(row_count, model_width).astype(jnp.float32)
    normed_one, scaled_one, inverse_one = layer_norm(
        inputs, gain_one.astype(jnp.float32), shift_one.astype(jnp.float32)
    )
    normed_one = normed_one.astype(jnp.bfloat16)
    qv_float = bias_qv.astype(jnp.float32)
    bias_full = jnp.concatenate(
        [qv_float[:model_width], jnp.zeros((model_width,), jnp.float32), qv_float[model_width:]]
    )
    qkv_low = (jnp.dot(normed_one, w_qkv, preferred_element_type=jnp.float32) + bias_full).astype(
        jnp.bfloat16
    )
    qkv_items = qkv_low.reshape(item_count, slot_count, 3 * model_width)
    mixed_items, log_totals = lax.map(attend_forward, (qkv_items, lengths, blocks))
    mixed_low = mixed_items.reshape(row_count, model_width)
    middle = (
        inputs
        + jnp.dot(mixed_low, w_out, preferred_element_type=jnp.float32)
        + bias_out.astype(jnp.float32)
    )
    normed_two, scaled_two, inverse_two = layer_norm(
        middle, gain_two.astype(jnp.float32), shift_two.astype(jnp.float32)
    )
    normed_two = normed_two.astype(jnp.bfloat16)
    pre_active = jnp.dot(normed_two, w_up, preferred_element_type=jnp.float32) + bias_up.astype(
        jnp.float32
    )
    active, gelu_back = jax.vjp(partial(jax.nn.gelu, approximate=True), pre_active)
    active_low = active.astype(jnp.bfloat16)
    branch_mlp = jnp.dot(active_low, w_down, preferred_element_type=jnp.float32) + bias_down.astype(
        jnp.float32
    )
    slot_ids = lax.broadcasted_iota(jnp.int32, (item_count, slot_count), 1)
    valid_rows = (slot_ids < lengths[:, None]).astype(jnp.float32).reshape(row_count, 1)
    output = (
        ((middle + branch_mlp) * valid_rows)
        .astype(jnp.bfloat16)
        .reshape(item_count, slot_count, model_width)
    )
    back_weights = fetch(shards)
    (
        back_gain_one,
        back_shift_one,
        back_qkv,
        back_bias_qv,
        back_out,
        back_bias_out,
        back_gain_two,
        back_shift_two,
        back_up,
        back_bias_up,
        back_down,
        back_bias_down,
    ) = back_weights
    d_result = cotangent.reshape(row_count, model_width).astype(jnp.float32) * valid_rows
    d_lower = d_result.astype(jnp.bfloat16)
    grad_bias_down = jnp.sum(d_lower.astype(jnp.float32), axis=0)
    grad_down = jnp.einsum("rf,rd->fd", active_low, d_lower, preferred_element_type=jnp.float32)
    d_active = jnp.einsum("rd,fd->rf", d_lower, back_down, preferred_element_type=jnp.float32)
    d_pre = gelu_back(d_active)[0].astype(jnp.bfloat16)
    grad_bias_up = jnp.sum(d_pre.astype(jnp.float32), axis=0)
    grad_up = jnp.einsum("rd,rf->df", normed_two, d_pre, preferred_element_type=jnp.float32)
    d_normed_two = jnp.einsum("rf,df->rd", d_pre, back_up, preferred_element_type=jnp.float32)
    d_inner, grad_gain_two, grad_shift_two = norm_back(
        d_normed_two, scaled_two, inverse_two, back_gain_two.astype(jnp.float32)
    )
    d_middle = d_result + d_inner
    d_branch = d_middle.astype(jnp.bfloat16)
    grad_bias_out = jnp.sum(d_branch.astype(jnp.float32), axis=0)
    grad_out = jnp.einsum("rd,re->de", mixed_low, d_branch, preferred_element_type=jnp.float32)
    d_mixed = jnp.einsum(
        "re,de->rd", d_branch, back_out, preferred_element_type=jnp.float32
    ).astype(jnp.bfloat16)
    d_qkv = lax.map(
        attend_backward,
        (
            qkv_items,
            lengths,
            blocks,
            log_totals,
            d_mixed.reshape(item_count, slot_count, model_width),
        ),
    )
    d_qkv = d_qkv.reshape(row_count, 3 * model_width)
    column_sums = jnp.sum(d_qkv.astype(jnp.float32), axis=0)
    grad_bias_qv = jnp.concatenate([column_sums[:model_width], column_sums[2 * model_width :]])
    grad_qkv = jnp.einsum("rd,re->de", normed_one, d_qkv, preferred_element_type=jnp.float32)
    d_normed_one = jnp.einsum("re,de->rd", d_qkv, back_qkv, preferred_element_type=jnp.float32)
    d_first, grad_gain_one, grad_shift_one = norm_back(
        d_normed_one, scaled_one, inverse_one, back_gain_one.astype(jnp.float32)
    )
    input_grad = (d_middle + d_first).reshape(item_count, slot_count, model_width)
    owned = reduce_grads(
        (
            grad_gain_one,
            grad_shift_one,
            grad_qkv,
            grad_bias_qv,
            grad_out,
            grad_bias_out,
            grad_gain_two,
            grad_shift_two,
            grad_up,
            grad_bias_up,
            grad_down,
            grad_bias_down,
        )
    )
    return (output, input_grad) + owned


def solution(mesh):
    return jax.shard_map(
        body,
        mesh=mesh,
        in_specs=(
            P(("wide", "narrow"), None, None),
            P(("wide", "narrow")),
            P(("wide", "narrow"), None),
            P(("wide", "narrow")),
            P(("wide", "narrow")),
            P(("wide", "narrow"), None),
            P(("wide", "narrow")),
            P(("wide", "narrow"), None),
            P(("wide", "narrow")),
            P(("wide", "narrow")),
            P(("wide", "narrow")),
            P(("wide", "narrow"), None),
            P(("wide", "narrow")),
            P(("wide", "narrow"), None),
            P(("wide", "narrow")),
            P(("wide", "narrow"), None, None),
        ),
        out_specs=(
            P(("wide", "narrow"), None, None),
            P(("wide", "narrow"), None, None),
            P(("wide", "narrow")),
            P(("wide", "narrow")),
            P(("wide", "narrow"), None),
            P(("wide", "narrow")),
            P(("wide", "narrow"), None),
            P(("wide", "narrow")),
            P(("wide", "narrow")),
            P(("wide", "narrow")),
            P(("wide", "narrow"), None),
            P(("wide", "narrow")),
            P(("wide", "narrow"), None),
            P(("wide", "narrow")),
        ),
        check_vma=False,
    )
```

profile of v0, /device:TPU:0, one launch (start us, length us, event | category | flops | bytes accessed | tf_op | source)
XLA Modules:
  0.0 839.9 jit_solution(17000271752070816200)
XLA Ops:
  16.5 42.7 %all-reduce.17 = (bf16[1536]{0:T(1024)(128)(2,1)S(1)}, bf16[768]{0:T(1024)(128)(2,1)S(1)}, bf16[768]{0:T(1024)(128)(2,1)S(1)}, bf16[768]{0:T(1024)(128)(2,1)S(1)...) all-reduce(bf16[1536]{0:T(1024)(128)(2,1)S(1)} %dynamic-update-slic, ...), channel_id=1, replica_groups=mesh['wide'=8,'narrow'=4] {'wide','narrow'}, use_global_device_ids=true, to_apply=%add.2 | all-reduce | flops 9216 | bytes 36864
  73.9 10.0 %fusion.22 = bf16[1200,2304]{1,0:T(8,128)(2,1)} fusion(bf16[768,2304]{1,0:T(8,128)(2,1)} %all-gather.5.cloned.1.call-done, f32[2304]{0:T(1024)S(1)} %pad_maximum_fusion, f32[1200,768]{1,0:T(8,128)} %fusion.26, f32[768]{0:T(1024)S(1)} %convert_element_type.143, f32[768]{0:T(1024)S(1)} %convert_element_type.142), kind=kOutput, calls=%fused_computation.47 | convolution fusion | flops 4255027200 | bytes 12770304 | tf_op jit(solution)/shard_map/dot_general | solution.py:221
  83.9 8.8 %copy.52 = bf16[2,600,2304]{1,2,0:T(8,128)(2,1)} copy(bf16[2,600,2304]{2,1,0:T(8,128)(2,1)} %bitcast.156) | data formatting | bytes 11059200 | tf_op jit(solution)/shard_map/while | solution.py:225
  92.8 78.2 %while.22 = (s32[]{:T(128)}, bf16[2,600,768]{2,1,0:T(8,128)(2,1)}, f32[2,12,600,1]{2,1,3,0:T(8,128)S(1)}, bf16[2,600,2304]{1,2,0:T(8,128)(2,1)}, s32[2,600]{1,0:T(2,128)S(1)}, /*index=5*/s32[2]{0:T(128)S(1)}, s32[]{:T(128)}) while((s32[]{:T(128)}, bf16[2,600,768]{2,1,0:T(8,128)(2,1)}, f32[2,12,600,1]{2,1,3,0:T(8,128)S(1)}, ...), condition=%wide.region_5.6_spmd, body=%wide.region_2.5_spmd.sunk | while | flops 1158934144 | bytes 71987392 | solution.py:225
  98.1 8.2 fusion.99
  106.3 10.1 %fusion.100 = f32[12,600]{1,0:T(8,128)S(1)} fusion(f32[12,600,600]{1,2,0:T(8,128)} %get-tuple-element.288, f32[12,600]{1,0:T(8,128)S(1)} %get-tuple-element.289, pred[600,600]{0,1:T(8,128)(4,1)S(1)} %compare_and_fusion.4), kind=kLoop, calls=%fused_computation.4.clone.1 | loop fusion | flops 17272800 | bytes 17697600 | tf_op jit(solution)/shard_map/while/body/eval_jaxpr/reduce_sum | solution.py:56
  116.4 13.0 %fusion.101 = bf16[12,64,600]{2,1,0:T(8,128)(2,1)} fusion(bf16[600,12,64]{0,2,1:T(8,128)(2,1)} %bitcast.152, f32[12,600,600]{1,2,0:T(8,128)} %get-tuple-element.288, f32[12,600]{1,0:T(8,128)S(1)} %fusion.100, f32[12,600]{1,0:T(8,128)S(1)} %get-tuple-element.289, pred[600,600]{0,1:T(8,128)(4,1)S(1)} %compare_and_fusion.4), kind=kOutput, calls=%fused_computation.8.clone.1 | convolution fusion | flops 575020800 | bytes 19540800 | tf_op jit(solution)/shard_map/while/body/eval_jaxpr/hqk,khd->qhd/dot_general | solution.py:58
  136.9 8.2 fusion.99
  145.0 10.1 %fusion.100 = f32[12,600]{1,0:T(8,128)S(1)} fusion(f32[12,600,600]{1,2,0:T(8,128)} %get-tuple-element.288, f32[12,600]{1,0:T(8,128)S(1)} %get-tuple-element.289, pred[600,600]{0,1:T(8,128)(4,1)S(1)} %compare_and_fusion.4), kind=kLoop, calls=%fused_computation.4.clone.1 | loop fusion | flops 17272800 | bytes 17697600 | tf_op jit(solution)/shard_map/while/body/eval_jaxpr/reduce_sum | solution.py:56
  155.2 13.1 %fusion.101 = bf16[12,64,600]{2,1,0:T(8,128)(2,1)} fusion(bf16[600,12,64]{0,2,1:T(8,128)(2,1)} %bitcast.152, f32[12,600,600]{1,2,0:T(8,128)} %get-tuple-element.288, f32[12,600]{1,0:T(8,128)S(1)} %fusion.100, f32[12,600]{1,0:T(8,128)S(1)} %get-tuple-element.289, pred[600,600]{0,1:T(8,128)(4,1)S(1)} %compare_and_fusion.4), kind=kOutput, calls=%fused_computation.8.clone.1 | convolution fusion | flops 575020800 | bytes 19540800 | tf_op jit(solution)/shard_map/while/body/eval_jaxpr/hqk,khd->qhd/dot_general | solution.py:58
  177.2 18.0 %all-gather.9.cloned.1.call-done = bf16[768,3072]{1,0:T(8,128)(2,1)} async-done(((bf16[24,3072]{1,0:T(8,128)(2,1)}), bf16[768,3072]{1,0:T(8,128)(2,1)}) %all-gather.9.cloned.1.call-update) | async-done | bytes 4718608 | tf_op jit(solution)/shard_map/all_gather | solution.py:123
  195.2 12.4 %convolution_add_fusion.1 = f32[1200,3072]{1,0:T(8,128)} fusion(bf16[768,3072]{1,0:T(8,128)(2,1)} %all-gather.9.cloned.1.call-done, f32[3072]{0:T(1024)S(1)} %copy-done.35, f32[1200,768]{1,0:T(8,128)} %copy-done.5, f32[768]{0:T(1024)S(1)} %copy-done.37, f32[768]{0:T(1024)S(1)} %copy-done.32, f32[1200]{0:T(1024)S(1)} %add_rsqrt_fusion, ...), kind=kOutput, calls=%fused_computation.45 | convolution fusion | flops 5670604800 | bytes 23178624 | tf_op jit(solution)/shard_map/dot_general | solution.py:236
  207.6 52.9 %all-gather.11.cloned.1.call-done = bf16[3072,768]{1,0:T(8,128)(2,1)} async-done(((bf16[96,768]{1,0:T(8,128)(2,1)}), bf16[3072,768]{1,0:T(8,128)(2,1)}) %all-gather.11.cloned.1.call-update) | async-done | bytes 4718608 | tf_op jit(solution)/shard_map/all_gather | solution.py:125
  260.4 18.6 %convert_reduce_fusion = (f32[3072]{0:T(1024)}, bf16[1200,3072]{1,0:T(8,128)(2,1)}) fusion(f32[1200,3072]{1,0:T(8,128)} %convolution_add_fusion.1, bf16[1200,768]{1,0:T(8,128)(2,1)S(1)} %copy-done.10, bf16[3072,768]{1,0:T(8,128)(2,1)} %all-gather.11.cloned.1.call-done), kind=kOutput, calls=%fused_computation.42 | convolution fusion | flops 5743408128 | bytes 28692480 | tf_op jit(solution)/shard_map/rd,fd->rf/dot_general | solution.py:270
  279.1 10.6 %multiply_reduce_fusion.1 = (f32[768]{0:T(1024)}, f32[1200]{0:T(1024)S(1)}, f32[1200]{0:T(1024)S(1)}, f32[768]{0:T(1024)}, f32[1200,768]{1,0:T(8,128)S(1)}) fusion(f32[1200,768]{1,0:T(8,128)S(1)} %copy-done.6, f32[1200]{0:T(1024)S(1)} %add_rsqrt_fusion, f32[1200]{0:T(1024)S(1)} %broadcast_multiply_fusion.4, f32[768]{0:T(1024)S(1)} %copy-done.32, ...), kind=kOutput, calls=%fused_computation.59 | convolution fusion | flops 5670600704 | bytes 19492608 | tf_op jit(solution)/shard_map/rf,df->rd/dot_general | solution.py:274
  302.2 116.2 %while.23 = (s32[]{:T(128)}, bf16[2,600,2304]{1,2,0:T(8,128)(2,1)}, bf16[2,600,2304]{1,2,0:T(8,128)(2,1)}, s32[2,600]{1,0:T(2,128)S(1)}, s32[2]{0:T(128)S(1)}, /...) while((s32[]{:T(128)}, bf16[2,600,2304]{1,2,0:T(8,128)(2,1)}, ...), condition=%wide.region_12.13_spmd, body=%wide.region_10.12_spmd.sunk | while | flops 2840911872 | bytes 160925648 | solution.py:285
  308.5 8.2 fusion.113
  316.7 11.0 %fusion.114 = bf16[12,64,600]{2,1,0:T(8,128)(2,1)S(1)} fusion(bf16[600,12,64]{0,2,1:T(8,128)(2,1)S(1)} %bitcast.148, f32[12,600,600]{1,2,0:T(8,128)} %fusion.113, f32[12,600]{1,0:T(8,128)S(1)} %dynamic-slice_bitcast_fusion.8, pred[600,600]{0,1:T(8,128)(4,1)S(1)} %compare_and_fusion.5), kind=kOutput, calls=%fused_computation.26.clone.1 | convolution fusion | flops 570700800 | bytes 19512000 | tf_op jit(solution)/shard_map/while/body/eval_jaxpr/hqk,qhd->khd/dot_general | solution.py:77
  327.7 13.2 %multiply_reduce_fusion.10 = (f32[12,600]{1,0:T(8,128)S(1)}, f32[12,600,600]{1,2,0:T(8,128)}) fusion(f32[12,600,600]{1,2,0:T(8,128)} %fusion.113, f32[12,600]{1,0:T(8,128)S(1)} %dynamic-slice_bitcast_fusion.8, pred[600,600]{0,1:T(8,128)(4,1)S(1)} %compare_and_fusion.5, bf16[600,12,64]{0,2,1:T(8,128)(2,1)S(1)} %bitcast.149, ...), kind=kOutput, calls=%fused_computation.16.clone.1 | convolution fusion | flops 574552832 | bytes 36820800 | tf_op jit(solution)/shard_map/while/body/eval_jaxpr/qhd,khd->hqk/dot_general | solution.py:78
  340.9 13.4 %multiply_convert_fusion.10 = bf16[12,600,600]{1,2,0:T(8,128)(2,1)S(1)} fusion(f32[12,600,600]{1,2,0:T(8,128)} %get-tuple-element.300, f32[12,600,600]{1,2,0:T(8,128)} %fusion.113, f32[12,600]{1,0:T(8,128)S(1)} %get-tuple-element.301, f32[12,600]{1,0:T(8,128)S(1)} %dynamic-slice_bitcast_fusion.8, pred[600,600]{0,1:T(8,128)(4,1)S(1)} %compare_and_fusion.5), kind=kLoop, calls=%fused_computation.15.clone.1 | loop fusion | flops 25920000 | bytes 43617600 | tf_op jit(solution)/shard_map/while/body/eval_jaxpr/convert_element_type | solution.py:79
  374.7 10.8 %fusion.114 = bf16[12,64,600]{2,1,0:T(8,128)(2,1)S(1)} fusion(bf16[600,12,64]{0,2,1:T(8,128)(2,1)S(1)} %bitcast.148, f32[12,600,600]{1,2,0:T(8,128)} %fusion.113, f32[12,600]{1,0:T(8,128)S(1)} %dynamic-slice_bitcast_fusion.8, pred[600,600]{0,1:T(8,128)(4,1)S(1)} %compare_and_fusion.5), kind=kOutput, calls=%fused_computation.26.clone.1 | convolution fusion | flops 570700800 | bytes 19512000 | tf_op jit(solution)/shard_map/while/body/eval_jaxpr/hqk,qhd->khd/dot_general | solution.py:77
  385.6 13.1 %multiply_reduce_fusion.10 = (f32[12,600]{1,0:T(8,128)S(1)}, f32[12,600,600]{1,2,0:T(8,128)}) fusion(f32[12,600,600]{1,2,0:T(8,128)} %fusion.113, f32[12,600]{1,0:T(8,128)S(1)} %dynamic-slice_bitcast_fusion.8, pred[600,600]{0,1:T(8,128)(4,1)S(1)} %compare_and_fusion.5, bf16[600,12,64]{0,2,1:T(8,128)(2,1)S(1)} %bitcast.149, ...), kind=kOutput, calls=%fused_computation.16.clone.1 | convolution fusion | flops 574552832 | bytes 36820800 | tf_op jit(solution)/shard_map/while/body/eval_jaxpr/qhd,khd->hqk/dot_general | solution.py:78
  398.7 13.0 %multiply_convert_fusion.10 = bf16[12,600,600]{1,2,0:T(8,128)(2,1)S(1)} fusion(f32[12,600,600]{1,2,0:T(8,128)} %get-tuple-element.300, f32[12,600,600]{1,2,0:T(8,128)} %fusion.113, f32[12,600]{1,0:T(8,128)S(1)} %get-tuple-element.301, f32[12,600]{1,0:T(8,128)S(1)} %dynamic-slice_bitcast_fusion.8, pred[600,600]{0,1:T(8,128)(4,1)S(1)} %compare_and_fusion.5), kind=kLoop, calls=%fused_computation.15.clone.1 | loop fusion | flops 25920000 | bytes 43617600 | tf_op jit(solution)/shard_map/while/body/eval_jaxpr/convert_element_type | solution.py:79
  418.4 11.7 %convolution_bitcast_fusion = f32[768,2304]{1,0:T(8,128)} fusion(bf16[2,600,2304]{1,2,0:T(8,128)(2,1)} %get-tuple-element.86, bf16[2,600,768]{2,1,0:T(8,128)(2,1)} %param.20, f32[768]{0:T(1024)S(1)} %copy-done.40, f32[768]{0:T(1024)S(1)} %copy-done.31, f32[2,600]{1,0:T(2,128)S(1)} %copy-done.29, f32[2,600]{1,0:T(2,128)S(1)} %copy-done.25), kind=kOutput, calls=%fused_computation.48 | convolution fusion | flops 4252262400 | bytes 14466432 | tf_op jit(solution)/shard_map/rd,re->de/dot_general | solution.py:298
  431.6 13.5 %fusion.39 = f32[3072,768]{1,0:T(8,128)} fusion(bf16[1200,768]{1,0:T(8,128)(2,1)S(1)} %copy-done.11, f32[1200,3072]{1,0:T(8,128)} %convolution_add_fusion.1), kind=kOutput, calls=%fused_computation.99 | convolution fusion | flops 5695488000 | bytes 26025984 | tf_op jit(solution)/shard_map/rf,rd->fd/dot_general | solution.py:269
  445.8 13.0 %fusion.38 = f32[768,3072]{1,0:T(8,128)} fusion(bf16[1200,3072]{1,0:T(8,128)(2,1)} %get-tuple-element.199, f32[1200,768]{1,0:T(8,128)} %copy-done.5, f32[768]{0:T(1024)S(1)} %copy-done.38, f32[768]{0:T(1024)S(1)} %copy-done.33, f32[1200]{0:T(1024)S(1)} %copy-done.27, f32[1200]{0:T(1024)S(1)} %copy-done.14), kind=kOutput, calls=%fused_computation.98 | convolution fusion | flops 5666918400 | bytes 20512128 | tf_op jit(solution)/shard_map/rd,rf->df/dot_general | solution.py:273
  460.9 8.9 %copy.56 = bf16[2,600,2304]{2,1,0:T(8,128)(2,1)} copy(bf16[2,600,2304]{1,2,0:T(8,128)(2,1)} %get-tuple-element.86) | data formatting | bytes 11059200 | tf_op jit(solution)/shard_map/while | solution.py:285
  474.2 10.7 %fusion.40 = (f32[768]{0:T(1024)S(1)}, f32[768]{0:T(1024)S(1)}, f32[1200]{0:T(1024)S(1)}, f32[1200]{0:T(1024)S(1)}, f32[1200,768]{1,0:T(8,128)}) fusion(f32[1200]{0:T(1024)S(1)} %copy-done.21, f32[1200]{0:T(1024)S(1)} %copy-done.16, bf16[2,600,768]{2,1,0:T(8,128)(2,1)S(1)} %copy-done.2, f32[1200,768]{1,0:T(8,128)S(1)} %copy-done.9, ...), kind=kOutput, calls=%fused_computation.100 | convolution fusion | flops 4255944704 | bytes 18312960 | tf_op jit(solution)/shard_map/re,de->rd/dot_general | solution.py:299
  484.9 42.3 %all-reduce.16 = (f32[768]{0:T(1024)S(1)}, f32[768]{0:T(1024)S(1)}, f32[1536]{0:T(1024)S(1)}, f32[768]{0:T(1024)S(1)}, f32[768]{0:T(1024)S(1)}, /*index=5*/f32[7...) all-reduce(f32[768]{0:T(1024)S(1)} %get-tuple-element.133, ...), channel_id=2, replica_groups=mesh['wide'=8,'narrow'=4] {'wide','narrow'}, use_global_device_ids=true, to_apply=%region_16.17.clone | all-reduce | flops 9216 | bytes 73728
  537.2 14.2 %fusion.28 = bf16[1200,768]{1,0:T(8,128)(2,1)} fusion(f32[1200,768]{1,0:T(8,128)S(1)} %copy-done.7, bf16[3072,768]{1,0:T(8,128)(2,1)} %all-gather.11.cloned.1.call-done, f32[1200]{0:T(1024)S(1)} %copy-done.19, f32[768]{0:T(1024)S(1)} %convert_element_type.153, f32[1200,3072]{1,0:T(8,128)} %convolution_add_fusion.1), kind=kOutput, calls=%fused_computation.75 | convolution fusion | flops 5699174400 | bytes 25001664 | tf_op jit(solution)/shard_map/dot_general | solution.py:241
  551.4 139.3 %reduce-scatter.11.cloned.1.call-done = f32[96,768]{1,0:T(8,128)} async-done(((f32[3072,768]{1,0:T(8,128)}), f32[96,768]{1,0:T(8,128)}) %reduce-scatter.11.cloned.1.call-update) | async-done | bytes 294928 | tf_op jit(solution)/shard_map/reduce_scatter | solution.py:157
  690.7 142.1 %reduce-scatter.9.cloned.1.call-done = f32[24,3072]{1,0:T(8,128)} async-done(((f32[768,3072]{1,0:T(8,128)}), f32[24,3072]{1,0:T(8,128)}) %reduce-scatter.9.cloned.1.call-update) | async-done | bytes 294928 | tf_op jit(solution)/shard_map/reduce_scatter | solution.py:155
  (239 shorter events, 108.3 us)
Async XLA Ops:
  7.3 66.6 %all-gather.5.cloned.1.call-start = ((), (), s32[]{:S(2)}) async-start(), calls=%async_computation.4 | async-start | bytes 3649536 | tf_op jit(solution)/shard_map/all_gather | solution.py:117
  8.0 163.0 %all-gather.7.cloned.1.call-start = ((), (), s32[]{:S(2)}) async-start(), calls=%async_computation.5 | async-start | bytes 1216512 | tf_op jit(solution)/shard_map/all_gather | solution.py:119
  8.8 186.4 %all-gather.9.cloned.1.call-start = ((), (), s32[]{:S(2)}) async-start(), calls=%async_computation.6 | async-start | bytes 4866048 | tf_op jit(solution)/shard_map/all_gather | solution.py:123
  9.5 250.9 %all-gather.11.cloned.1.call-start = ((), (), s32[]{:S(2)}) async-start(), calls=%async_computation.7 | async-start | bytes 4866048 | tf_op jit(solution)/shard_map/all_gather | solution.py:125
  10.1 541.4 %reduce-scatter.7.cloned.1.call-start = ((), (), s32[]{:S(2)}) async-start(), calls=%async_computation.9 | async-start | bytes 2433024 | tf_op jit(solution)/shard_map/reduce_scatter | solution.py:151
  10.1 54.8 %copy-start = (bf16[2,600,768]{2,1,0:T(8,128)(2,1)S(1)}, bf16[2,600,768]{2,1,0:T(8,128)(2,1)}, u32[]{:S(2)}) copy-start(bf16[2,600,768]{2,1,0:T(8,128)(2,1)} %param.20) | copy-start | bytes 5529604
  14.4 52.9 %copy-start.15 = (f32[1200]{0:T(1024)}, f32[1200]{0:T(1024)S(1)}, u32[]{:S(2)}) copy-start(f32[1200]{0:T(1024)S(1)} %div.35) | copy-start | bytes 14404
  14.5 46.5 %copy-start.22 = (f32[2,600]{1,0:T(2,128)}, f32[2,600]{1,0:T(2,128)S(1)}, u32[]{:S(2)}) copy-start(f32[2,600]{1,0:T(2,128)S(1)} %compare_convert_fusion) | copy-start | bytes 14404
  14.6 52.7 %copy-start.17 = (f32[1200]{0:T(1024)}, f32[1200]{0:T(1024)S(1)}, u32[]{:S(2)}) copy-start(f32[1200]{0:T(1024)S(1)} %reshape.369) | copy-start | bytes 14404
  14.6 52.7 %copy-start.28 = (f32[2,600]{1,0:T(2,128)}, f32[2,600]{1,0:T(2,128)S(1)}, u32[]{:S(2)}) copy-start(f32[2,600]{1,0:T(2,128)S(1)} %add_rsqrt_fusion.1) | copy-start | bytes 14404
  59.2 14.7 %copy-start.30 = (f32[768]{0:T(1024)}, f32[768]{0:T(1024)S(1)}, u32[]{:S(2)}) copy-start(f32[768]{0:T(1024)S(1)} %convert_element_type.142) | copy-start | bytes 9220
  59.8 14.1 %copy-start.39 = (f32[768]{0:T(1024)}, f32[768]{0:T(1024)S(1)}, u32[]{:S(2)}) copy-start(f32[768]{0:T(1024)S(1)} %convert_element_type.143) | copy-start | bytes 9220
  92.7 78.3 %copy-start.1 = (bf16[2,600,768]{2,1,0:T(8,128)(2,1)S(1)}, bf16[2,600,768]{2,1,0:T(8,128)(2,1)}, u32[]{:S(2)}) copy-start(bf16[2,600,768]{2,1,0:T(8,128)(2,1)} %param.20) | copy-start | bytes 5529604
  92.7 78.3 %copy-start.41 = (f32[768]{0:T(1024)S(1)}, f32[768]{0:T(1024)}, u32[]{:S(2)}) copy-start(f32[768]{0:T(1024)} %convert_element_type.147) | copy-start | bytes 9220
  174.7 20.4 %copy-start.32 = (f32[768]{0:T(1024)S(1)}, f32[768]{0:T(1024)}, u32[]{:S(2)}) copy-start(f32[768]{0:T(1024)} %convert_element_type.148) | copy-start | bytes 9220
  174.7 20.4 %copy-start.35 = (f32[3072]{0:T(1024)S(1)}, f32[3072]{0:T(1024)}, u32[]{:S(2)}) copy-start(f32[3072]{0:T(1024)} %convert_element_type.151) | copy-start | bytes 36868
  174.7 20.4 %copy-start.37 = (f32[768]{0:T(1024)S(1)}, f32[768]{0:T(1024)}, u32[]{:S(2)}) copy-start(f32[768]{0:T(1024)} %convert_element_type.149) | copy-start | bytes 9220
  174.8 114.9 %copy-start.13 = (f32[1200]{0:T(1024)}, f32[1200]{0:T(1024)S(1)}, u32[]{:S(2)}) copy-start(f32[1200]{0:T(1024)S(1)} %broadcast_multiply_fusion.4) | copy-start | bytes 14404
  177.2 112.5 %copy-start.26 = (f32[1200]{0:T(1024)}, f32[1200]{0:T(1024)S(1)}, u32[]{:S(2)}) copy-start(f32[1200]{0:T(1024)S(1)} %add_rsqrt_fusion) | copy-start | bytes 14404
  177.2 83.2 %copy-start.10 = (bf16[1200,768]{1,0:T(8,128)(2,1)S(1)}, bf16[1200,768]{1,0:T(8,128)(2,1)}, u32[]{:S(2)}) copy-start(bf16[1200,768]{1,0:T(8,128)(2,1)} %fusion.27) | copy-start | bytes 5529604
  260.4 18.6 %copy-start.6 = (f32[1200,768]{1,0:T(8,128)S(1)}, f32[1200,768]{1,0:T(8,128)}, u32[]{:S(2)}) copy-start(f32[1200,768]{1,0:T(8,128)} %copy-done.5) | copy-start | bytes 11059204
  260.4 18.6 %copy-start.46 = (bf16[768,3072]{1,0:T(8,128)(2,1)S(1)}, bf16[768,3072]{1,0:T(8,128)(2,1)}, u32[]{:S(2)}) copy-start(bf16[768,3072]{1,0:T(8,128)(2,1)} %all-gather.9.cloned.1.call-done) | copy-start | bytes 14155780
  297.2 254.3 %reduce-scatter.5.cloned.1.call-start = ((), (), s32[]{:S(2)}) async-start(), calls=%async_computation.8 | async-start | bytes 7299072 | tf_op jit(solution)/shard_map/reduce_scatter | solution.py:149
  302.2 116.2 %copy-start.25 = (f32[2,600]{1,0:T(2,128)S(1)}, f32[2,600]{1,0:T(2,128)}, u32[]{:S(2)}) copy-start(f32[2,600]{1,0:T(2,128)} %copy-done.24) | copy-start | bytes 14404
  302.2 116.2 %copy-start.29 = (f32[2,600]{1,0:T(2,128)S(1)}, f32[2,600]{1,0:T(2,128)}, u32[]{:S(2)}) copy-start(f32[2,600]{1,0:T(2,128)} %copy-done.28) | copy-start | bytes 14404
  302.2 116.2 %copy-start.31 = (f32[768]{0:T(1024)S(1)}, f32[768]{0:T(1024)}, u32[]{:S(2)}) copy-start(f32[768]{0:T(1024)} %copy-done.30) | copy-start | bytes 9220
  302.2 116.2 %copy-start.40 = (f32[768]{0:T(1024)S(1)}, f32[768]{0:T(1024)}, u32[]{:S(2)}) copy-start(f32[768]{0:T(1024)} %copy-done.39) | copy-start | bytes 9220
  430.1 260.7 %reduce-scatter.11.cloned.1.call-start = ((), (), s32[]{:S(2)}) async-start(), calls=%async_computation.11 | async-start | bytes 9732096 | tf_op jit(solution)/shard_map/reduce_scatter | solution.py:157
  445.1 387.7 %reduce-scatter.9.cloned.1.call-start = ((), (), s32[]{:S(2)}) async-start(), calls=%async_computation.10 | async-start | bytes 9732096 | tf_op jit(solution)/shard_map/reduce_scatter | solution.py:155
  474.2 10.7 %copy-start.34 = (f32[768]{0:T(1024)S(1)}, f32[768]{0:T(1024)}, u32[]{:S(2)}) copy-start(f32[768]{0:T(1024)} %get-tuple-element.178) | copy-start | bytes 9220
  474.2 10.7 %copy-start.36 = (f32[3072]{0:T(1024)S(1)}, f32[3072]{0:T(1024)}, u32[]{:S(2)}) copy-start(f32[3072]{0:T(1024)} %get-tuple-element.198) | copy-start | bytes 36868
  474.2 10.7 %copy-start.42 = (f32[768]{0:T(1024)S(1)}, f32[768]{0:T(1024)}, u32[]{:S(2)}) copy-start(f32[768]{0:T(1024)} %get-tuple-element.126) | copy-start | bytes 9220
  (33 other events, 169.1 us)
Sparse Core Ops, SparseCore 0:
  11.0 62.8 all-gather.4
  76.8 52.8 all-gather.6
  132.6 62.5 all-gather.8
  197.9 62.4 all-gather.10
  297.3 97.8 reduce-scatter.6
  430.2 119.0 reduce-scatter.4
  555.8 134.9 reduce-scatter.10
  698.2 134.5 reduce-scatter.8
where the time goes:
time: 848 us; the launch traced here: 840 us
  waiting for transfers between devices  361 us (43%)
  matrix products  243 us (29%)
  blocking collectives  85.1 us (10%)
  other arithmetic  78.9 us (9%)
  local copies, waits for them, and re-layouts  55.3 us (7%)
  between operations  14.9 us (2%)
    reduce_scatter x1, waiting for transfers between devices, reduce_grads(): lax.psum_scatter(w_up, ('wide', 'narrow'), scatter_dimension=0, tiled=True)  142 us
    reduce_scatter x1, waiting for transfers between devices, reduce_grads(): lax.psum_scatter(w_down, ('wide', 'narrow'), scatter_dimension=0, tiled=T...  139 us
    unnamed x2, blocking collectives  85.1 us
    all_gather x1, waiting for transfers between devices, fetch(): lax.all_gather(w_down, ('wide', 'narrow'), axis=0, tiled=True)  52.9 us
    dot_general x4, matrix products, score_table(): jnp.einsum('qhd,khd->hqk', queries, key_rows, preferred_element_type=jnp....  32.6 us
    convert_element_type x2, other arithmetic, attend_backward(): (probs * (d_probs - jnp.sum(probs * d_probs, axis=-1, keepdims=True))).as...  26.5 us
    dot_general x2, matrix products, attend_backward(): jnp.einsum('qhd,khd->hqk', d_heads, value_rows, preferred_element_type=jn...  26.3 us
    dot_general x2, matrix products, attend_forward(): jnp.einsum('hqk,khd->qhd', probs_low, head_split(qkv_item, 2), preferred_...  26 us
  transfers between devices with their start and end apart: 8, of which 5 were waited for; matrix products, arithmetic and copies ran while one was open for 40% of the time, Pallas kernels for 0%

commit v1 on v0

--- a/solution.py
+++ b/solution.py
@@ -9,6 +9,28 @@
 HEAD = 64
 norm_epsilon = 1e-05
 masked_score = -1e30
+
+
+def in_order(blocks, dim):
+    blocks = jnp.moveaxis(blocks, 0, dim)
+    dims = blocks.shape
+    return blocks.reshape(*dims[:dim], dims[dim] * dims[dim + 1], *dims[dim + 2 :])
+
+
+def doubled(x, axis):
+    size = lax.axis_size(axis)
+    pieces = x[None]
+    for level in range(size.bit_length() - 1):
+        bit = 1 << level
+        other = lax.ppermute(pieces, axis, [(i, i ^ bit) for i in range(size)])
+        both = jnp.stack([pieces, other])
+        upper = lax.axis_index(axis) >> level & 1
+        pieces = jnp.where(upper == 0, both, both[::-1]).reshape(-1, *x.shape)
+    return pieces
+
+
+def gather_by_bits(shard, axis, dim):
+    return in_order(doubled(shard, axis), dim)
 
 
 def layer_norm(values, gain, shift):
@@ -122,7 +144,7 @@
         lax.all_gather(shift_two, ("wide", "narrow"), axis=0, tiled=True),
         lax.all_gather(w_up, ("wide", "narrow"), axis=0, tiled=True),
         lax.all_gather(bias_up, ("wide", "narrow"), axis=0, tiled=True),
-        lax.all_gather(w_down, ("wide", "narrow"), axis=0, tiled=True),
+        gather_by_bits(w_down, ("wide", "narrow"), 0),
         lax.all_gather(bias_down, ("wide", "narrow"), axis=0, tiled=True),
     )
     return whole_set

time: 848 us -> 929 us (1.096)
  blocking collectives: 85.1 us -> 165 us
  waiting for transfers between devices: 361 us -> 346 us
  other arithmetic: 78.9 us -> 88.4 us
    unnamed x2, blocking collectives: 85.1 us -> 165 us
    ppermute x0 -> x5, waiting for transfers between devices: none -> 61.6 us  [doubled(): other = lax.ppermute(pieces, axis, [(i, i ^ bit) for i in range(size)])]
    all_gather x1 -> x0, waiting for transfers between devices: 52.9 us -> none  [fetch(): lax.all_gather(w_down, ('wide', 'narrow'), axis=0, tiled=True)]
    all_gather x1, waiting for transfers between devices: 18 us -> 0.02 us  [fetch(): lax.all_gather(w_up, ('wide', 'narrow'), axis=0, tiled=True)]
  transfers between devices with their start and end apart: 8 -> 12, of which waited for: 5 -> 7; matrix products, arithmetic and copies ran while one was open for 40% -> 36% of each run, Pallas kernels for 0% -> 0%
where the time goes in v1:
time: 929 us; the launch traced here: 924 us
  waiting for transfers between devices  346 us (37%)
  matrix products  243 us (26%)
  blocking collectives  165 us (18%)
  other arithmetic  88.4 us (10%)
  local copies, waits for them, and re-layouts  56 us (6%)
  between operations  14.9 us (2%)
  starting transfers between devices  9.47 us (1%)
    unnamed x2, blocking collectives  165 us
    reduce_scatter x1, waiting for transfers between devices, reduce_grads(): lax.psum_scatter(w_up, ('wide', 'narrow'), scatter_dimension=0, tiled=True)  142 us
    reduce_scatter x1, waiting for transfers between devices, reduce_grads(): lax.psum_scatter(w_down, ('wide', 'narrow'), scatter_dimension=0, tiled=T...  141 us
    ppermute x5, waiting for transfers between devices, doubled(): other = lax.ppermute(pieces, axis, [(i, i ^ bit) for i in range(size)])  61.6 us
    dot_general x4, matrix products, score_table(): jnp.einsum('qhd,khd->hqk', queries, key_rows, preferred_element_type=jnp....  32.7 us
    convert_element_type x2, other arithmetic, attend_backward(): (probs * (d_probs - jnp.sum(probs * d_probs, axis=-1, keepdims=True))).as...  26.5 us
    dot_general x2, matrix products, attend_backward(): jnp.einsum('qhd,khd->hqk', d_heads, value_rows, preferred_element_type=jn...  26.3 us
    dot_general x2, matrix products, attend_forward(): jnp.einsum('hqk,khd->qhd', probs_low, head_split(qkv_item, 2), preferred_...  26.1 us
  transfers between devices with their start and end apart: 12, of which 7 were waited for; matrix products, arithmetic and copies ran while one was open for 36% of the time, Pallas kernels for 0%

profile of v1, /device:TPU:0, one launch (start us, length us, event | category | flops | bytes accessed | tf_op | source)
XLA Modules:
  0.0 923.9 jit_solution(2114445409657151508)
XLA Ops:
  22.9 13.9 %collective-permute-done.2 = bf16[4,96,768]{2,1,0:T(8,128)(2,1)S(1)} collective-permute-done((bf16[4,96,768]{2,1,0:T(8,128)(2,1)S(1)}, bf16[4,96,768]{2,1,0:T(8,128)(2,1)S(1)}, u32[]{:S(2)}, u32[]{:S(2)}) %collective-permute-start.2) | collective-permute-done | bytes 589856 | tf_op jit(solution)/shard_map/ppermute | solution.py:25
  38.8 39.2 %collective-permute-done.3 = bf16[8,96,768]{2,1,0:T(8,128)(2,1)S(1)} collective-permute-done((bf16[8,96,768]{2,1,0:T(8,128)(2,1)S(1)}, bf16[8,96,768]{2,1,0:T(8,128)(2,1)S(1)}, u32[]{:S(2)}, u32[]{:S(2)}) %collective-permute-start.3) | collective-permute-done | bytes 1179680 | tf_op jit(solution)/shard_map/ppermute | solution.py:25
  87.4 123.6 %all-reduce.17 = (bf16[1536]{0:T(1024)(128)(2,1)S(1)}, bf16[768]{0:T(1024)(128)(2,1)S(1)}, bf16[768]{0:T(1024)(128)(2,1)S(1)}, bf16[768]{0:T(1024)(128)(2,1)S(1)...) all-reduce(bf16[1536]{0:T(1024)(128)(2,1)S(1)} %dynamic-update-slic, ...), channel_id=1, replica_groups=mesh['wide'=8,'narrow'=4] {'wide','narrow'}, use_global_device_ids=true, to_apply=%add.2 | all-reduce | flops 9216 | bytes 36864
  227.4 10.0 %fusion.22 = bf16[1200,2304]{1,0:T(8,128)(2,1)} fusion(bf16[768,2304]{1,0:T(8,128)(2,1)} %all-gather.4.cloned.1.call-done, f32[2304]{0:T(1024)S(1)} %pad_maximum_fusion.5, f32[1200,768]{1,0:T(8,128)} %fusion.26, f32[768]{0:T(1024)S(1)} %convert_element_type.147, f32[768]{0:T(1024)S(1)} %convert_element_type.146), kind=kOutput, calls=%fused_computation.47 | convolution fusion | flops 4255027200 | bytes 12770304 | tf_op jit(solution)/shard_map/dot_general | solution.py:243
  237.5 8.8 copy.52
  246.3 78.5 %while.22 = (s32[]{:T(128)}, bf16[2,600,768]{2,1,0:T(8,128)(2,1)}, f32[2,12,600,1]{2,1,3,0:T(8,128)S(1)}, bf16[2,600,2304]{1,2,0:T(8,128)(2,1)}, s32[2,600]{1,0:T(2,128)S(1)}, /*index=5*/s32[2]{0:T(128)S(1)}, s32[]{:T(128)}) while((s32[]{:T(128)}, bf16[2,600,768]{2,1,0:T(8,128)(2,1)}, f32[2,12,600,1]{2,1,3,0:T(8,128)S(1)}, ...), condition=%wide.region_5.6_spmd, body=%wide.region_2.5_spmd.sunk | while | flops 1158934144 | bytes 71987392 | solution.py:247
  251.4 8.2 fusion.101
  259.6 10.3 %fusion.102 = f32[12,600]{1,0:T(8,128)S(1)} fusion(f32[12,600,600]{1,2,0:T(8,128)} %get-tuple-element.293, f32[12,600]{1,0:T(8,128)S(1)} %get-tuple-element.294, pred[600,600]{0,1:T(8,128)(4,1)S(1)} %compare_and_fusion.4), kind=kLoop, calls=%fused_computation.4.clone.1 | loop fusion | flops 17272800 | bytes 17697600 | tf_op jit(solution)/shard_map/while/body/eval_jaxpr/reduce_sum | solution.py:78
  269.9 13.1 %fusion.103 = bf16[12,64,600]{2,1,0:T(8,128)(2,1)} fusion(bf16[600,12,64]{0,2,1:T(8,128)(2,1)} %bitcast.171, f32[12,600,600]{1,2,0:T(8,128)} %get-tuple-element.293, f32[12,600]{1,0:T(8,128)S(1)} %fusion.102, f32[12,600]{1,0:T(8,128)S(1)} %get-tuple-element.294, pred[600,600]{0,1:T(8,128)(4,1)S(1)} %compare_and_fusion.4), kind=kOutput, calls=%fused_computation.8.clone.1 | convolution fusion | flops 575020800 | bytes 19540800 | tf_op jit(solution)/shard_map/while/body/eval_jaxpr/hqk,khd->qhd/dot_general | solution.py:80
  290.5 8.2 fusion.101
  298.7 10.1 %fusion.102 = f32[12,600]{1,0:T(8,128)S(1)} fusion(f32[12,600,600]{1,2,0:T(8,128)} %get-tuple-element.293, f32[12,600]{1,0:T(8,128)S(1)} %get-tuple-element.294, pred[600,600]{0,1:T(8,128)(4,1)S(1)} %compare_and_fusion.4), kind=kLoop, calls=%fused_computation.4.clone.1 | loop fusion | flops 17272800 | bytes 17697600 | tf_op jit(solution)/shard_map/while/body/eval_jaxpr/reduce_sum | solution.py:78
  308.8 13.0 %fusion.103 = bf16[12,64,600]{2,1,0:T(8,128)(2,1)} fusion(bf16[600,12,64]{0,2,1:T(8,128)(2,1)} %bitcast.171, f32[12,600,600]{1,2,0:T(8,128)} %get-tuple-element.293, f32[12,600]{1,0:T(8,128)S(1)} %fusion.102, f32[12,600]{1,0:T(8,128)S(1)} %get-tuple-element.294, pred[600,600]{0,1:T(8,128)(4,1)S(1)} %compare_and_fusion.4), kind=kOutput, calls=%fused_computation.8.clone.1 | convolution fusion | flops 575020800 | bytes 19540800 | tf_op jit(solution)/shard_map/while/body/eval_jaxpr/hqk,khd->qhd/dot_general | solution.py:80
  331.0 12.5 %convolution_add_fusion.1 = f32[1200,3072]{1,0:T(8,128)} fusion(bf16[768,3072]{1,0:T(8,128)(2,1)} %all-gather.8.cloned.1.call-done, f32[3072]{0:T(1024)S(1)} %copy-done.33, f32[1200,768]{1,0:T(8,128)} %copy-done.3, f32[768]{0:T(1024)S(1)} %copy-done.35, f32[768]{0:T(1024)S(1)} %copy-done.29, f32[1200]{0:T(1024)S(1)} %add_rsqrt_fusion, ...), kind=kOutput, calls=%fused_computation.45 | convolution fusion | flops 5670604800 | bytes 23178624 | tf_op jit(solution)/shard_map/dot_general | solution.py:258
  343.5 18.6 %convert_reduce_fusion = (f32[3072]{0:T(1024)}, bf16[1200,3072]{1,0:T(8,128)(2,1)}) fusion(f32[1200,3072]{1,0:T(8,128)} %convolution_add_fusion.1, bf16[1200,768]{1,0:T(8,128)(2,1)S(1)} %bitcast.183, bf16[3072,768]{1,0:T(8,128)(2,1)} %bitcast.176), kind=kOutput, calls=%fused_computation.42 | convolution fusion | flops 5743408128 | bytes 28692480 | tf_op jit(solution)/shard_map/rd,fd->rf/dot_general | solution.py:292
  362.2 10.6 %multiply_reduce_fusion.1 = (f32[768]{0:T(1024)}, f32[1200]{0:T(1024)S(1)}, f32[1200]{0:T(1024)S(1)}, f32[768]{0:T(1024)}, f32[1200,768]{1,0:T(8,128)S(1)}) fusion(f32[1200,768]{1,0:T(8,128)S(1)} %copy-done.4, f32[1200]{0:T(1024)S(1)} %add_rsqrt_fusion, f32[1200]{0:T(1024)S(1)} %broadcast_multiply_fusion.4, f32[768]{0:T(1024)S(1)} %copy-done.29, ...), kind=kOutput, calls=%fused_computation.60 | convolution fusion | flops 5670600704 | bytes 19492608 | tf_op jit(solution)/shard_map/rf,df->rd/dot_general | solution.py:296
  386.3 116.0 %while.23 = (s32[]{:T(128)}, bf16[2,600,2304]{1,2,0:T(8,128)(2,1)}, bf16[2,600,2304]{1,2,0:T(8,128)(2,1)}, s32[2,600]{1,0:T(2,128)S(1)}, s32[2]{0:T(128)S(1)}, /...) while((s32[]{:T(128)}, bf16[2,600,2304]{1,2,0:T(8,128)(2,1)}, ...), condition=%wide.region_12.13_spmd, body=%wide.region_10.12_spmd.sunk | while | flops 2840911872 | bytes 160925648 | solution.py:307
  392.5 8.2 fusion.115
  400.6 11.0 %fusion.116 = bf16[12,64,600]{2,1,0:T(8,128)(2,1)S(1)} fusion(bf16[600,12,64]{0,2,1:T(8,128)(2,1)S(1)} %bitcast.167, f32[12,600,600]{1,2,0:T(8,128)} %fusion.115, f32[12,600]{1,0:T(8,128)S(1)} %dynamic-slice_bitcast_fusion.8, pred[600,600]{0,1:T(8,128)(4,1)S(1)} %compare_and_fusion.5), kind=kOutput, calls=%fused_computation.26.clone.1 | convolution fusion | flops 570700800 | bytes 19512000 | tf_op jit(solution)/shard_map/while/body/eval_jaxpr/hqk,qhd->khd/dot_general | solution.py:99
  411.7 13.2 %multiply_reduce_fusion.10 = (f32[12,600]{1,0:T(8,128)S(1)}, f32[12,600,600]{1,2,0:T(8,128)}) fusion(f32[12,600,600]{1,2,0:T(8,128)} %fusion.115, f32[12,600]{1,0:T(8,128)S(1)} %dynamic-slice_bitcast_fusion.8, pred[600,600]{0,1:T(8,128)(4,1)S(1)} %compare_and_fusion.5, bf16[600,12,64]{0,2,1:T(8,128)(2,1)S(1)} %bitcast.168, ...), kind=kOutput, calls=%fused_computation.16.clone.1 | convolution fusion | flops 574552832 | bytes 36820800 | tf_op jit(solution)/shard_map/while/body/eval_jaxpr/qhd,khd->hqk/dot_general | solution.py:100
  424.9 13.4 %multiply_convert_fusion.11 = bf16[12,600,600]{1,2,0:T(8,128)(2,1)S(1)} fusion(f32[12,600,600]{1,2,0:T(8,128)} %get-tuple-element.305, f32[12,600,600]{1,2,0:T(8,128)} %fusion.115, f32[12,600]{1,0:T(8,128)S(1)} %get-tuple-element.306, f32[12,600]{1,0:T(8,128)S(1)} %dynamic-slice_bitcast_fusion.8, pred[600,600]{0,1:T(8,128)(4,1)S(1)} %compare_and_fusion.5), kind=kLoop, calls=%fused_computation.15.clone.1 | loop fusion | flops 25920000 | bytes 43617600 | tf_op jit(solution)/shard_map/while/body/eval_jaxpr/convert_element_type | solution.py:101
  458.7 10.8 %fusion.116 = bf16[12,64,600]{2,1,0:T(8,128)(2,1)S(1)} fusion(bf16[600,12,64]{0,2,1:T(8,128)(2,1)S(1)} %bitcast.167, f32[12,600,600]{1,2,0:T(8,128)} %fusion.115, f32[12,600]{1,0:T(8,128)S(1)} %dynamic-slice_bitcast_fusion.8, pred[600,600]{0,1:T(8,128)(4,1)S(1)} %compare_and_fusion.5), kind=kOutput, calls=%fused_computation.26.clone.1 | convolution fusion | flops 570700800 | bytes 19512000 | tf_op jit(solution)/shard_map/while/body/eval_jaxpr/hqk,qhd->khd/dot_general | solution.py:99
  469.5 13.1 %multiply_reduce_fusion.10 = (f32[12,600]{1,0:T(8,128)S(1)}, f32[12,600,600]{1,2,0:T(8,128)}) fusion(f32[12,600,600]{1,2,0:T(8,128)} %fusion.115, f32[12,600]{1,0:T(8,128)S(1)} %dynamic-slice_bitcast_fusion.8, pred[600,600]{0,1:T(8,128)(4,1)S(1)} %compare_and_fusion.5, bf16[600,12,64]{0,2,1:T(8,128)(2,1)S(1)} %bitcast.168, ...), kind=kOutput, calls=%fused_computation.16.clone.1 | convolution fusion | flops 574552832 | bytes 36820800 | tf_op jit(solution)/shard_map/while/body/eval_jaxpr/qhd,khd->hqk/dot_general | solution.py:100
  482.7 13.0 %multiply_convert_fusion.11 = bf16[12,600,600]{1,2,0:T(8,128)(2,1)S(1)} fusion(f32[12,600,600]{1,2,0:T(8,128)} %get-tuple-element.305, f32[12,600,600]{1,2,0:T(8,128)} %fusion.115, f32[12,600]{1,0:T(8,128)S(1)} %get-tuple-element.306, f32[12,600]{1,0:T(8,128)S(1)} %dynamic-slice_bitcast_fusion.8, pred[600,600]{0,1:T(8,128)(4,1)S(1)} %compare_and_fusion.5), kind=kLoop, calls=%fused_computation.15.clone.1 | loop fusion | flops 25920000 | bytes 43617600 | tf_op jit(solution)/shard_map/while/body/eval_jaxpr/convert_element_type | solution.py:101
  502.4 11.7 %convolution_bitcast_fusion = f32[768,2304]{1,0:T(8,128)} fusion(bf16[2,600,2304]{1,2,0:T(8,128)(2,1)} %get-tuple-element.86, bf16[2,600,768]{2,1,0:T(8,128)(2,1)} %param.20, f32[768]{0:T(1024)S(1)} %copy-done.38, f32[768]{0:T(1024)S(1)} %copy-done.28, f32[2,600]{1,0:T(2,128)S(1)} %copy-done.26, f32[2,600]{1,0:T(2,128)S(1)} %copy-done.20), kind=kOutput, calls=%fused_computation.49 | convolution fusion | flops 4252262400 | bytes 14466432 | tf_op jit(solution)/shard_map/rd,re->de/dot_general | solution.py:320
  515.5 13.5 %fusion.41 = f32[3072,768]{1,0:T(8,128)} fusion(bf16[1200,768]{1,0:T(8,128)(2,1)S(1)} %copy-done.9, f32[1200,3072]{1,0:T(8,128)} %convolution_add_fusion.1), kind=kOutput, calls=%fused_computation.111 | convolution fusion | flops 5695488000 | bytes 26025984 | tf_op jit(solution)/shard_map/rf,rd->fd/dot_general | solution.py:291
  529.8 13.2 %fusion.40 = f32[768,3072]{1,0:T(8,128)} fusion(bf16[1200,3072]{1,0:T(8,128)(2,1)} %get-tuple-element.204, f32[1200,768]{1,0:T(8,128)} %copy-done.3, f32[768]{0:T(1024)S(1)} %copy-done.36, f32[768]{0:T(1024)S(1)} %copy-done.30, f32[1200]{0:T(1024)S(1)} %copy-done.24, f32[1200]{0:T(1024)S(1)} %copy-done.14), kind=kOutput, calls=%fused_computation.110 | convolution fusion | flops 5666918400 | bytes 20512128 | tf_op jit(solution)/shard_map/rd,rf->df/dot_general | solution.py:295
  543.7 9.0 copy.56
  557.2 10.7 %fusion.42 = (f32[768]{0:T(1024)S(1)}, f32[768]{0:T(1024)S(1)}, f32[1200]{0:T(1024)S(1)}, f32[1200]{0:T(1024)S(1)}, f32[1200,768]{1,0:T(8,128)}) fusion(f32[1200]{0:T(1024)S(1)} %copy-done.18, f32[1200]{0:T(1024)S(1)} %copy-done.16, bf16[2,600,768]{2,1,0:T(8,128)(2,1)S(1)} %copy-done.2, f32[1200,768]{1,0:T(8,128)S(1)} %copy-done.8, ...), kind=kOutput, calls=%fused_computation.112 | convolution fusion | flops 4255944704 | bytes 18312960 | tf_op jit(solution)/shard_map/re,de->rd/dot_general | solution.py:321
  567.9 41.0 %all-reduce.16 = (f32[768]{0:T(1024)S(1)}, f32[768]{0:T(1024)S(1)}, f32[1536]{0:T(1024)S(1)}, f32[768]{0:T(1024)S(1)}, f32[768]{0:T(1024)S(1)}, /*index=5*/f32[7...) all-reduce(f32[768]{0:T(1024)S(1)} %get-tuple-element.133, ...), channel_id=2, replica_groups=mesh['wide'=8,'narrow'=4] {'wide','narrow'}, use_global_device_ids=true, to_apply=%region_16.17.clone | all-reduce | flops 9216 | bytes 73728
  618.8 14.4 %fusion.28 = bf16[1200,768]{1,0:T(8,128)(2,1)} fusion(f32[1200,768]{1,0:T(8,128)S(1)} %copy-done.5, bf16[3072,768]{1,0:T(8,128)(2,1)} %bitcast.177, f32[1200]{0:T(1024)S(1)} %copy-done.22, f32[768]{0:T(1024)S(1)} %convert_element_type.157, f32[1200,3072]{1,0:T(8,128)} %convolution_add_fusion.1), kind=kOutput, calls=%fused_computation.78 | convolution fusion | flops 5699174400 | bytes 25001664 | tf_op jit(solution)/shard_map/dot_general | solution.py:263
  633.6 141.3 %reduce-scatter.11.cloned.1.call-done = f32[96,768]{1,0:T(8,128)} async-done(((f32[3072,768]{1,0:T(8,128)}), f32[96,768]{1,0:T(8,128)}) %reduce-scatter.11.cloned.1.call-update) | async-done | bytes 294928 | tf_op jit(solution)/shard_map/reduce_scatter | solution.py:179
  774.9 142.0 %reduce-scatter.9.cloned.1.call-done = f32[24,3072]{1,0:T(8,128)} async-done(((f32[768,3072]{1,0:T(8,128)}), f32[24,3072]{1,0:T(8,128)}) %reduce-scatter.9.cloned.1.call-update) | async-done | bytes 294928 | tf_op jit(solution)/shard_map/reduce_scatter | solution.py:177
  (254 shorter events, 127.9 us)
Async XLA Ops:
  7.2 220.3 %all-gather.4.cloned.1.call-start = ((), (), s32[]{:S(2)}) async-start(), calls=%async_computation.4 | async-start | bytes 3649536 | tf_op jit(solution)/shard_map/all_gather | solution.py:139
  7.9 316.9 %all-gather.6.cloned.1.call-start = ((), (), s32[]{:S(2)}) async-start(), calls=%async_computation.5 | async-start | bytes 1216512 | tf_op jit(solution)/shard_map/all_gather | solution.py:141
  8.0 1.7 collective-permute-start
  10.7 10.2 %collective-permute-start.1 = (bf16[2,96,768]{2,1,0:T(8,128)(2,1)S(1)}, bf16[2,96,768]{2,1,0:T(8,128)(2,1)S(1)}, u32[]{:S(2)}, u32[]{:S(2)}) collective-permute-start(bf16[2,96,768]{2,1,0:T(8,128)(2,1)S(1)} %get-tuple-element.194), channel_id=1, source_target_pairs={{0,2},{1,3},{2,0},{3,1},{4,6},{5,7},{6,4},{7,5},{8,10},{9,11},{10,... | collective-permute-start | bytes 884744 | tf_op jit(solution)/shard_map/ppermute | solution.py:25
  13.6 317.3 %all-gather.8.cloned.1.call-start = ((), (), s32[]{:S(2)}) async-start(), calls=%async_computation.6 | async-start | bytes 4866048 | tf_op jit(solution)/shard_map/all_gather | solution.py:145
  21.1 15.7 %collective-permute-start.2 = (bf16[4,96,768]{2,1,0:T(8,128)(2,1)S(1)}, bf16[4,96,768]{2,1,0:T(8,128)(2,1)S(1)}, u32[]{:S(2)}, u32[]{:S(2)}) collective-permute-start(bf16[4,96,768]{2,1,0:T(8,128)(2,1)S(1)} %bitcast.181), channel_id=1, source_target_pairs={{0,4},{1,5},{2,6},{3,7},{4,0},{5,1},{6,2},{7,3},{8,12},{9,13},{10,... | collective-permute-start | bytes 1769480 | tf_op jit(solution)/shard_map/ppermute | solution.py:25
  37.2 40.9 %collective-permute-start.3 = (bf16[8,96,768]{2,1,0:T(8,128)(2,1)S(1)}, bf16[8,96,768]{2,1,0:T(8,128)(2,1)S(1)}, u32[]{:S(2)}, u32[]{:S(2)}) collective-permute-start(bf16[8,96,768]{2,1,0:T(8,128)(2,1)S(1)} %bitcast.178), channel_id=1, source_target_pairs={{0,8},{1,9},{2,10},{3,11},{4,12},{5,13},{6,14},{7,15},{8,0},{9,1},... | collective-permute-start | bytes 3538952 | tf_op jit(solution)/shard_map/ppermute | solution.py:25
  38.8 594.4 %reduce-scatter.7.cloned.1.call-start = ((), (), s32[]{:S(2)}) async-start(), calls=%async_computation.8 | async-start | bytes 2433024 | tf_op jit(solution)/shard_map/reduce_scatter | solution.py:173
  80.8 132.9 %copy-start.43 = (s32[2]{0:T(128)S(1)}, s32[2]{0:T(128)}, u32[]{:S(2)}) copy-start(s32[2]{0:T(128)} %param.21) | copy-start | bytes 28
  82.7 138.7 %collective-permute-start.4 = (bf16[16,96,768]{2,1,0:T(8,128)(2,1)}, bf16[16,96,768]{2,1,0:T(8,128)(2,1)}, u32[]{:S(2)}, u32[]{:S(2)}) collective-permute-start(bf16[16,96,768]{2,1,0:T(8,128)(2,1)} %bitcast.37), channel_id=1, source_target_pairs={{0,16},{1,17},{2,18},{3,19},{4,20},{5,21},{6,22},{7,23},{8,24},{9,... | collective-permute-start | bytes 7077896 | tf_op jit(solution)/shard_map/ppermute | solution.py:25
  211.0 16.5 %copy-start.27 = (f32[768]{0:T(1024)}, f32[768]{0:T(1024)S(1)}, u32[]{:S(2)}) copy-start(f32[768]{0:T(1024)S(1)} %convert_element_type.146) | copy-start | bytes 9220
  211.6 15.9 %copy-start.37 = (f32[768]{0:T(1024)}, f32[768]{0:T(1024)S(1)}, u32[]{:S(2)}) copy-start(f32[768]{0:T(1024)S(1)} %convert_element_type.147) | copy-start | bytes 9220
  246.3 78.6 %copy-start.1 = (bf16[2,600,768]{2,1,0:T(8,128)(2,1)S(1)}, bf16[2,600,768]{2,1,0:T(8,128)(2,1)}, u32[]{:S(2)}) copy-start(bf16[2,600,768]{2,1,0:T(8,128)(2,1)} %param.20) | copy-start | bytes 5529604
  246.3 78.6 %copy-start.39 = (f32[768]{0:T(1024)S(1)}, f32[768]{0:T(1024)}, u32[]{:S(2)}) copy-start(f32[768]{0:T(1024)} %convert_element_type.151) | copy-start | bytes 9220
  328.6 44.2 %copy-start.13 = (f32[1200]{0:T(1024)}, f32[1200]{0:T(1024)S(1)}, u32[]{:S(2)}) copy-start(f32[1200]{0:T(1024)S(1)} %broadcast_multiply_fusion.4) | copy-start | bytes 14404
  330.9 41.9 %copy-start.23 = (f32[1200]{0:T(1024)}, f32[1200]{0:T(1024)S(1)}, u32[]{:S(2)}) copy-start(f32[1200]{0:T(1024)S(1)} %add_rsqrt_fusion) | copy-start | bytes 14404
  330.9 12.6 %copy-start.10 = (bf16[2,600,768]{2,1,0:T(8,128)(2,1)S(1)}, bf16[2,600,768]{2,1,0:T(8,128)(2,1)}, u32[]{:S(2)}) copy-start(bf16[2,600,768]{2,1,0:T(8,128)(2,1)} %get-tuple-element.179) | copy-start | bytes 5529604
  331.0 31.2 %slice-start = ((s8[4718592]{0:T(1024)(128)(4,1)}), s8[4194304]{0:T(1024)(128)(4,1)S(1)}, s32[]{:S(2)}) async-start(s8[4718592]{0:T(1024)(128)(4,1)} %bitcast.190), calls=%async_computation.11 | async-start | bytes 8388608
  343.5 18.7 %copy-start.4 = (f32[1200,768]{1,0:T(8,128)S(1)}, f32[1200,768]{1,0:T(8,128)}, u32[]{:S(2)}) copy-start(f32[1200,768]{1,0:T(8,128)} %copy-done.3) | copy-start | bytes 11059204
  343.5 18.7 %slice-start.1 = ((s8[4718592]{0:T(1024)(128)(4,1)}), s8[524288]{0:T(1024)(128)(4,1)S(1)}, s32[]{:S(2)}) async-start(s8[4718592]{0:T(1024)(128)(4,1)} %bitcast.190), calls=%async_computation.12 | async-start | bytes 1048576
  381.3 252.3 %reduce-scatter.5.cloned.1.call-start = ((), (), s32[]{:S(2)}) async-start(), calls=%async_computation.7 | async-start | bytes 7299072 | tf_op jit(solution)/shard_map/reduce_scatter | solution.py:171
  386.3 116.0 %copy-start.20 = (f32[2,600]{1,0:T(2,128)S(1)}, f32[2,600]{1,0:T(2,128)}, u32[]{:S(2)}) copy-start(f32[2,600]{1,0:T(2,128)} %copy-done.19) | copy-start | bytes 14404
  386.3 116.0 %copy-start.26 = (f32[2,600]{1,0:T(2,128)S(1)}, f32[2,600]{1,0:T(2,128)}, u32[]{:S(2)}) copy-start(f32[2,600]{1,0:T(2,128)} %copy-done.25) | copy-start | bytes 14404
  386.3 116.0 %copy-start.28 = (f32[768]{0:T(1024)S(1)}, f32[768]{0:T(1024)}, u32[]{:S(2)}) copy-start(f32[768]{0:T(1024)} %copy-done.27) | copy-start | bytes 9220
  386.3 116.0 %copy-start.38 = (f32[768]{0:T(1024)S(1)}, f32[768]{0:T(1024)}, u32[]{:S(2)}) copy-start(f32[768]{0:T(1024)} %copy-done.37) | copy-start | bytes 9220
  514.1 260.8 %reduce-scatter.11.cloned.1.call-start = ((), (), s32[]{:S(2)}) async-start(), calls=%async_computation.10 | async-start | bytes 9732096 | tf_op jit(solution)/shard_map/reduce_scatter | solution.py:179
  529.1 387.8 %reduce-scatter.9.cloned.1.call-start = ((), (), s32[]{:S(2)}) async-start(), calls=%async_computation.9 | async-start | bytes 9732096 | tf_op jit(solution)/shard_map/reduce_scatter | solution.py:177
  557.1 10.7 %copy-start.31 = (f32[768]{0:T(1024)S(1)}, f32[768]{0:T(1024)}, u32[]{:S(2)}) copy-start(f32[768]{0:T(1024)} %get-tuple-element.180) | copy-start | bytes 9220
  557.1 10.7 %copy-start.32 = (f32[768]{0:T(1024)S(1)}, f32[768]{0:T(1024)}, u32[]{:S(2)}) copy-start(f32[768]{0:T(1024)} %get-tuple-element.178) | copy-start | bytes 9220
  557.1 10.7 %copy-start.34 = (f32[3072]{0:T(1024)S(1)}, f32[3072]{0:T(1024)}, u32[]{:S(2)}) copy-start(f32[3072]{0:T(1024)} %get-tuple-element.203) | copy-start | bytes 36868
  557.1 10.7 %copy-start.40 = (f32[768]{0:T(1024)S(1)}, f32[768]{0:T(1024)}, u32[]{:S(2)}) copy-start(f32[768]{0:T(1024)} %get-tuple-element.126) | copy-start | bytes 9220
  557.1 10.7 %copy-start.41 = (f32[768]{0:T(1024)S(1)}, f32[768]{0:T(1024)}, u32[]{:S(2)}) copy-start(f32[768]{0:T(1024)} %get-tuple-element.131) | copy-start | bytes 9220
  (36 other events, 158.5 us)
Sparse Core Ops, SparseCore 0:
  10.9 68.2 all-gather.3
  82.1 124.5 all-gather.5
  209.6 62.4 all-gather.7
  381.5 97.9 reduce-scatter.6
  514.2 119.3 reduce-scatter.4
  639.9 134.9 reduce-scatter.10
  782.4 134.4 reduce-scatter.8
